TPU v7x, 128 devices: a whole 4x4x4 slice. The times are simulated.
128 devices in a mesh: samp: 32 (over y, x, core), slab: 4 (over z).
Axes of the slice: x: 4, y: 4, z: 4, core: 2. Of those that a mesh axis runs over, the one named last changes fastest.
Arguments:
- ld_blocks: bfloat16 [4, 64, 768, 768], P('slab', 'samp'), may hold values from -1 to 1, as said below
- marginal: float32 [4, 49152], P('slab', 'samp'), may hold values from -1.8 to 1.8
- normals: float32 [2, 4, 49152], P(None, 'slab', 'samp'), may hold values from -6 to 6
- block_len: int32 [64], P('samp'), may hold values from 1 to 768, 36864 in all
- scale_start: float32 [49152], P('samp'), may hold values from 0.2 to 5
- ancestry_weight: float32 [4], replicated, may hold values from 4 to 64
- dosage: bfloat16 [4096, 49152], P('samp', 'slab'), may hold values from 0 to 2
Outputs:
- effects: float32 [4, 49152], P('slab', 'samp')
- shrink: float32 [49152], P('samp')
- scores: float32 [4096, 4], P('samp', 'slab')
Inputs may be any that keep to these rules, and one draw needn't show every extreme that they name: `block_len`: the block lengths sum to 36864; the longest is exactly 768. `ld_blocks`: every block is symmetric with unit diagonal, and it and each of its leading principal submatrices is positive definite.
All inputs are finite; a program needn't handle non-finite values.
Results may differ from a plain program's by a relative error of at most 0.0031.
Values may be sent and summed in bfloat16 or wider, within the bound.
A program may use at most 128 MiB of HBM per device.

v0:
```python
import jax
import jax.numpy as jnp
from jax import lax
from jax.sharding import PartitionSpec as P

SWEEPS = 2
shape_total = 1.5
global_shrink = 0.01


def mean_rounded(stacked):
    total = stacked[:, 0]
    total = total + stacked[:, 1]
    return (total / stacked.shape[1]).astype(jnp.bfloat16)


def score_terms(columns, weights):
    product = lax.dot_general(
        columns, weights, (((1,), (1,)), ((), ())), preferred_element_type=jnp.float32
    )
    return (product, jnp.sum(weights.astype(jnp.float32), axis=1))


def per_device(ld_blocks, marginal, normals, block_len, scale_start, ancestry_weight, dosage):
    slot_count = ld_blocks.shape[1]
    block_size = ld_blocks.shape[2]
    ancestries = ancestry_weight.shape[0]
    own_index = lax.axis_index("slab")
    weight = lax.dynamic_index_in_dim(ancestry_weight, own_index, 0, keepdims=False)
    position = jnp.arange(block_size, dtype=jnp.int32)
    live_rows = (position[None, :] < block_len[:, None]).astype(jnp.float32)
    correlation = ld_blocks[0].astype(jnp.float32) * (live_rows[:, :, None] * live_rows[:, None, :])
    identity = jnp.eye(block_size, dtype=jnp.float32)
    targets = marginal[0].reshape(slot_count, block_size) * live_rows
    shrink = scale_start.reshape(slot_count, block_size)
    shrink_rate = shape_total / (shrink + global_shrink)
    variance = jnp.ones((), jnp.float32)
    local_live = jnp.sum(live_rows)
    live_total = local_live
    drawn = []
    for sweep_index in range(SWEEPS):
        inverse = 1.0 / shrink
        system = (
            correlation
            + identity[None, :, :] * (live_rows * inverse + (1.0 - live_rows))[:, None, :]
        )
        factor = jnp.linalg.cholesky(system)
        forward = lax.linalg.triangular_solve(
            factor, targets[:, :, None], left_side=True, lower=True
        )[:, :, 0]
        noise_level = jnp.sqrt(variance / weight)
        forward = (
            forward
            + noise_level * normals[sweep_index, 0].reshape(slot_count, block_size) * live_rows
        )
        effect = lax.linalg.triangular_solve(
            factor, forward[:, :, None], left_side=True, lower=True, transpose_a=True
        )[:, :, 0]
        fitted = jnp.einsum("sij,sj->si", correlation, effect, precision=lax.Precision.HIGHEST)
        misfit = targets - fitted
        stat_row = jnp.stack(
            [jnp.sum(misfit * misfit), jnp.sum(effect * effect * inverse * live_rows), local_live]
        )
        totals = lax.psum(stat_row, "samp")
        variance = (totals[0] + totals[1] + 1.0) / (totals[2] + 1.0)
        pooled = lax.psum(weight * effect * effect / variance, "slab")
        live_total = totals[2]
        shrink = (pooled + 1.0) / (2.0 + jnp.sqrt(4.0 + 2.0 * shrink_rate * (pooled + 1.0)))
        shrink_rate = shape_total / (shrink + global_shrink)
        drawn.append(effect.reshape(1, slot_count * block_size))
    total = drawn[0]
    sweep_index = 1
    total = total + drawn[sweep_index]
    effects = total / SWEEPS
    stacked = jnp.concatenate(drawn, axis=0)
    slab_count = lax.axis_size("slab")
    samp_count = lax.axis_size("samp")
    quarter = slot_count * block_size // slab_count
    spread = lax.all_gather(stacked, "samp", axis=1, tiled=True)
    layout = spread.reshape(1, SWEEPS, samp_count, slab_count, quarter)
    received = lax.all_to_all(layout, "slab", split_axis=3, concat_axis=0, tiled=True)
    weights = mean_rounded(received.reshape(ancestries, SWEEPS, samp_count * quarter))
    products, column_sums = score_terms(dosage, weights)
    partial_value = products - column_sums[None, :]
    scores = lax.psum_scatter(partial_value, "slab", scatter_dimension=1, tiled=True) / jnp.sqrt(
        live_total
    )
    return (effects, shrink.reshape(slot_count * block_size), scores)


def solution(mesh):
    return jax.shard_map(
        per_device,
        mesh=mesh,
        in_specs=(
            P("slab", "samp", None, None),
            P("slab", "samp"),
            P(None, "slab", "samp"),
            P("samp"),
            P("samp"),
            P(),
            P("samp", "slab"),
        ),
        out_specs=(P("slab", "samp"), P("samp"), P("samp", "slab")),
        check_vma=False,
    )
```

profile of v0, /device:TPU:0, one launch (start us, length us, event | category | flops | bytes accessed | tf_op | source)
XLA Modules:
  0.0 1182.4 jit_solution(14147899627568268930)
XLA Ops:
  28.3 23.5 %custom-call.57 = f32[2,128,128]{2,1,0:T(8,128)S(1)} custom-call(f32[2,128,128]{2,1,0:T(8,128)S(1)} %cholesky.662), custom_call_target="Cholesky" | custom-call | tf_op jit(solution)/shard_map/jit(cholesky)/cholesky | solution.py:47
  79.4 24.0 %custom-call.59 = f32[2,128,128]{2,1,0:T(8,128)S(1)} custom-call(f32[2,128,128]{2,1,0:T(8,128)S(1)} %cholesky.666), custom_call_target="Cholesky" | custom-call | tf_op jit(solution)/shard_map/jit(cholesky)/cholesky | solution.py:47
  129.7 23.5 %custom-call.61 = f32[2,128,128]{2,1,0:T(8,128)S(1)} custom-call(f32[2,128,128]{2,1,0:T(8,128)S(1)} %cholesky.671), custom_call_target="Cholesky" | custom-call | tf_op jit(solution)/shard_map/jit(cholesky)/cholesky | solution.py:47
  180.3 24.9 %custom-call.63 = f32[2,128,128]{2,1,0:T(8,128)} custom-call(f32[2,128,128]{2,1,0:T(8,128)} %cholesky.676), custom_call_target="Cholesky" | custom-call | tf_op jit(solution)/shard_map/jit(cholesky)/cholesky | solution.py:47
  206.8 21.1 %custom-call.64 = f32[2,1,128,128]{2,3,1,0:T(8,128)} custom-call(f32[2,1,128,128]{3,2,1,0:T(8,128)} %get-tuple-element.91), custom_call_target="InvertDiagBlocksLowerTriangular" | custom-call | tf_op jit(solution)/shard_map/jit(cholesky)/cholesky | solution.py:47
  233.1 24.5 %custom-call.65 = f32[2,128,128]{2,1,0:T(8,128)S(1)} custom-call(f32[2,128,128]{2,1,0:T(8,128)} %cholesky.681), custom_call_target="Cholesky" | custom-call | tf_op jit(solution)/shard_map/jit(cholesky)/cholesky | solution.py:47
  258.3 21.1 %custom-call.66 = f32[2,1,128,128]{2,3,1,0:T(8,128)} custom-call(f32[2,1,128,128]{3,2,1,0:T(8,128)} %get-tuple-element.89), custom_call_target="InvertDiagBlocksLowerTriangular" | custom-call | tf_op jit(solution)/shard_map/jit(cholesky)/cholesky | solution.py:47
  283.4 23.5 %custom-call.67 = f32[2,128,128]{2,1,0:T(8,128)S(1)} custom-call(f32[2,128,128]{2,1,0:T(8,128)S(1)} %convolution_subtract_fusion.9), custom_call_target="Cholesky" | custom-call | tf_op jit(solution)/shard_map/jit(cholesky)/cholesky | solution.py:47
  315.6 22.0 %while.8 = (s32[]{:T(128)}, f32[2,768,768]{2,1,0:T(8,128)}, s32[6,2]{0,1:T(2,128)S(1)}, f32[6,2,128,128]{3,2,0,1:T(8,128)}, s32[]{:T(128)}) while((s32[]{:T(128)}, f32[2,768,768]{2,1,0:T(8,128)}, s32[6,2]{0,1:T(2,128)S(1)}, f32[6,2,128,128]{3,2,0,1:T(8,128)}, s32[]{:T(128)}) %tuple.92), condition=%wide.while_cond.1, body=%wide.while_body.1.sunk | while | flops 2 | bytes 263777 | solution.py:56
  337.6 119.7 %custom-call.69 = f32[2,6,128,128]{2,3,1,0:T(8,128)} custom-call(f32[2,6,128,128]{3,2,1,0:T(8,128)} %bitcast.493), custom_call_target="InvertDiagBlocksLowerTriangular" | custom-call | tf_op jit(solution)/shard_map/triangular_solve/custom-call.12 | solution.py:56
  495.2 67.4 %psum.28 = f32[3]{0:T(128)S(1)} all-reduce(f32[3]{0:T(128)S(1)} %maximum_maximum_fusion), channel_id=1, replica_groups=mesh['samp'=32,'slab'=4] {'samp'}, use_global_device_ids=true, to_apply=%region_15.19 | all-reduce | flops 3 | bytes 24 | tf_op jit(solution)/shard_map/psum | solution.py:64
  596.8 23.5 %custom-call.70 = f32[2,128,128]{2,1,0:T(8,128)S(1)} custom-call(f32[2,128,128]{2,1,0:T(8,128)S(1)} %cholesky.685), custom_call_target="Cholesky" | custom-call | tf_op jit(solution)/shard_map/jit(cholesky)/cholesky | solution.py:47
  647.9 23.7 %custom-call.72 = f32[2,128,128]{2,1,0:T(8,128)S(1)} custom-call(f32[2,128,128]{2,1,0:T(8,128)S(1)} %cholesky.689), custom_call_target="Cholesky" | custom-call | tf_op jit(solution)/shard_map/jit(cholesky)/cholesky | solution.py:47
  697.8 23.5 %custom-call.74 = f32[2,128,128]{2,1,0:T(8,128)S(1)} custom-call(f32[2,128,128]{2,1,0:T(8,128)S(1)} %cholesky.694), custom_call_target="Cholesky" | custom-call | tf_op jit(solution)/shard_map/jit(cholesky)/cholesky | solution.py:47
  722.1 20.9 %custom-call.75 = f32[2,1,128,128]{2,3,1,0:T(8,128)S(1)} custom-call(f32[2,1,128,128]{3,2,1,0:T(8,128)} %get-tuple-element.84), custom_call_target="InvertDiagBlocksLowerTriangular" | custom-call | tf_op jit(solution)/shard_map/jit(cholesky)/cholesky | solution.py:47
  748.6 24.9 %custom-call.76 = f32[2,128,128]{2,1,0:T(8,128)} custom-call(f32[2,128,128]{2,1,0:T(8,128)} %cholesky.699), custom_call_target="Cholesky" | custom-call | tf_op jit(solution)/shard_map/jit(cholesky)/cholesky | solution.py:47
  775.2 21.1 %custom-call.77 = f32[2,1,128,128]{2,3,1,0:T(8,128)} custom-call(f32[2,1,128,128]{3,2,1,0:T(8,128)} %get-tuple-element.82), custom_call_target="InvertDiagBlocksLowerTriangular" | custom-call | tf_op jit(solution)/shard_map/jit(cholesky)/cholesky | solution.py:47
  801.4 24.4 %custom-call.78 = f32[2,128,128]{2,1,0:T(8,128)S(1)} custom-call(f32[2,128,128]{2,1,0:T(8,128)} %cholesky.704), custom_call_target="Cholesky" | custom-call | tf_op jit(solution)/shard_map/jit(cholesky)/cholesky | solution.py:47
  826.6 21.1 %custom-call.79 = f32[2,1,128,128]{2,3,1,0:T(8,128)} custom-call(f32[2,1,128,128]{3,2,1,0:T(8,128)} %get-tuple-element.80), custom_call_target="InvertDiagBlocksLowerTriangular" | custom-call | tf_op jit(solution)/shard_map/jit(cholesky)/cholesky | solution.py:47
  851.7 23.5 %custom-call.80 = f32[2,128,128]{2,1,0:T(8,128)S(1)} custom-call(f32[2,128,128]{2,1,0:T(8,128)S(1)} %convolution_subtract_fusion.8), custom_call_target="Cholesky" | custom-call | tf_op jit(solution)/shard_map/jit(cholesky)/cholesky | solution.py:47
  884.1 21.5 %while.9 = (s32[]{:T(128)}, f32[2,768,768]{2,1,0:T(8,128)}, s32[6,2]{0,1:T(2,128)S(1)}, f32[6,2,128,128]{3,2,0,1:T(8,128)}, s32[]{:T(128)}) while((s32[]{:T(128)}, f32[2,768,768]{2,1,0:T(8,128)}, s32[6,2]{0,1:T(2,128)S(1)}, f32[6,2,128,128]{3,2,0,1:T(8,128)}, s32[]{:T(128)}) %tuple.98), condition=%wide.while_cond.1.clone, body=%wide.while_body.1.clone.sunk | while | flops 2 | bytes 263777 | solution.py:56
  905.7 119.5 %custom-call.82 = f32[2,6,128,128]{2,3,1,0:T(8,128)} custom-call(f32[2,6,128,128]{3,2,1,0:T(8,128)} %bitcast.492), custom_call_target="InvertDiagBlocksLowerTriangular" | custom-call | tf_op jit(solution)/shard_map/triangular_solve/custom-call.12 | solution.py:56
  1054.7 22.0 %all_gather.3 = f32[2,49152]{1,0:T(2,128)S(1)} all-gather(f32[2,1536]{1,0:T(2,128)S(1)} %pad_maximum_fusion), channel_id=1, replica_groups=mesh['samp'=32,'slab'=4] {'samp'}, dimensions={1}, use_global_device_ids=true | all-gather | bytes 405504 | tf_op jit(solution)/shard_map/all_gather | solution.py:79
  1093.2 65.9 %psum.30 = f32[3]{0:T(128)} all-reduce(f32[3]{0:T(128)} %maximum_maximum_fusion.1), channel_id=1, replica_groups=mesh['samp'=32,'slab'=4] {'samp'}, use_global_device_ids=true, to_apply=%region_19.23 | all-reduce | flops 3 | bytes 24 | tf_op jit(solution)/shard_map/psum | solution.py:64
  (357 shorter events, 387.5 us)
Async XLA Ops:
  0.6 1167.7 %copy-start = (bf16[128,12288]{1,0:T(8,128)(2,1)S(1)}, bf16[128,12288]{1,0:T(8,128)(2,1)}, u32[]{:S(2)}) copy-start(bf16[128,12288]{1,0:T(8,128)(2,1)} %param.18) | copy-start | bytes 9437188
  51.8 27.6 %copy-start.7 = (f32[2,128,128]{2,1,0:T(8,128)}, f32[2,128,128]{2,1,0:T(8,128)S(1)}, u32[]{:S(2)}) copy-start(f32[2,128,128]{2,1,0:T(8,128)S(1)} %custom-call.57) | copy-start | bytes 393220
  103.4 71.1 %copy-start.9 = (f32[2,128,128]{2,1,0:T(8,128)}, f32[2,128,128]{2,1,0:T(8,128)S(1)}, u32[]{:S(2)}) copy-start(f32[2,128,128]{2,1,0:T(8,128)S(1)} %custom-call.59) | copy-start | bytes 393220
  309.2 148.1 %copy-start.33 = (s32[2]{0:T(128)S(1)}, s32[2]{0:T(128)}, u32[]{:S(2)}) copy-start(s32[2]{0:T(128)} %param.15) | copy-start | bytes 28
  309.2 148.1 %copy-start.36 = (f32[2,768,1]{1,0,2:T(2,128)S(1)}, f32[2,768,1]{1,0,2:T(2,128)}, u32[]{:S(2)}) copy-start(f32[2,768,1]{1,0,2:T(2,128)} %reshape_squeeze.13) | copy-start | bytes 18436
  314.5 157.3 %copy-start.41 = (f32[4]{0:T(128)S(1)}, f32[4]{0:T(128)}, u32[]{:S(2)}) copy-start(f32[4]{0:T(128)} %param.17) | copy-start | bytes 52
  314.5 158.8 %copy-start.37 = (f32[2,1,1536]{2,1,0:T(1,128)S(1)}, f32[2,1,1536]{2,1,0:T(1,128)}, u32[]{:S(2)}) copy-start(f32[2,1,1536]{2,1,0:T(1,128)} %param.14) | copy-start | bytes 36868
  314.5 173.2 %copy-start.14 = (f32[2,768]{1,0:T(2,128)S(1)}, f32[2,768]{1,0:T(2,128)}, u32[]{:S(2)}) copy-start(f32[2,768]{1,0:T(2,128)} %copy-done.13) | copy-start | bytes 18436
  337.6 154.8 %copy-start.16 = (s32[6,2]{0,1:T(2,128)}, s32[6,2]{0,1:T(2,128)S(1)}, u32[]{:S(2)}) copy-start(s32[6,2]{0,1:T(2,128)S(1)} %get-tuple-element.228) | copy-start | bytes 148
  457.4 30.3 %copy-start.29 = (f32[2,768,1]{1,0,2:T(2,128)}, f32[2,768,1]{1,0,2:T(2,128)S(1)}, u32[]{:S(2)}) copy-start(f32[2,768,1]{1,0,2:T(2,128)S(1)} %fusion.130) | copy-start | bytes 18436
  463.4 29.1 %copy-start.25 = (f32[2,768]{1,0:T(2,128)S(1)}, f32[2,768]{1,0:T(2,128)}, u32[]{:S(2)}) copy-start(f32[2,768]{1,0:T(2,128)} %copy-done.24) | copy-start | bytes 18436
  463.4 29.1 %copy-start.28 = (f32[2,768]{1,0:T(2,128)S(1)}, f32[2,768]{1,0:T(2,128)}, u32[]{:S(2)}) copy-start(f32[2,768]{1,0:T(2,128)} %reshape_squeeze.15) | copy-start | bytes 18436
  463.4 115.8 %copy-start.31 = (f32[1536]{0:T(1024)S(1)}, f32[1536]{0:T(1024)}, u32[]{:S(2)}) copy-start(f32[1536]{0:T(1024)} %get-tuple-element.97) | copy-start | bytes 18436
  487.8 96.5 %copy-start.18 = (f32[2,768,1]{1,0,2:T(2,128)}, f32[2,768,1]{1,0,2:T(2,128)S(1)}, u32[]{:S(2)}) copy-start(f32[2,768,1]{1,0,2:T(2,128)S(1)} %constant_dynamic-update-slice_fusion.16) | copy-start | bytes 18436
  620.3 27.6 %copy-start.8 = (f32[2,128,128]{2,1,0:T(8,128)}, f32[2,128,128]{2,1,0:T(8,128)S(1)}, u32[]{:S(2)}) copy-start(f32[2,128,128]{2,1,0:T(8,128)S(1)} %custom-call.70) | copy-start | bytes 393220
  671.6 71.3 %copy-start.10 = (f32[2,128,128]{2,1,0:T(8,128)}, f32[2,128,128]{2,1,0:T(8,128)S(1)}, u32[]{:S(2)}) copy-start(f32[2,128,128]{2,1,0:T(8,128)S(1)} %custom-call.72) | copy-start | bytes 393220
  877.8 147.4 %copy-start.39 = (f32[2,128,1]{1,0,2:T(2,128)S(1)}, f32[2,128,1]{1,0,2:T(2,128)}, u32[]{:S(2)}) copy-start(f32[2,128,1]{1,0,2:T(2,128)} %copy-done.38) | copy-start | bytes 3076
  877.8 149.7 %copy-start.30 = (f32[2,768,1]{1,0,2:T(2,128)S(1)}, f32[2,768,1]{1,0,2:T(2,128)}, u32[]{:S(2)}) copy-start(f32[2,768,1]{1,0,2:T(2,128)} %copy-done.29) | copy-start | bytes 18436
  883.1 156.5 %copy-start.34 = (s32[2]{0:T(128)S(1)}, s32[2]{0:T(128)}, u32[]{:S(2)}) copy-start(s32[2]{0:T(128)} %param.15) | copy-start | bytes 28
  883.1 156.5 %copy-start.35 = (f32[2,768,1]{1,0,2:T(2,128)S(1)}, f32[2,768,1]{1,0,2:T(2,128)}, u32[]{:S(2)}) copy-start(f32[2,768,1]{1,0,2:T(2,128)} %mul.175) | copy-start | bytes 18436
  883.1 170.9 %copy-start.19 = (f32[2,768,1]{1,0,2:T(2,128)S(1)}, f32[2,768,1]{1,0,2:T(2,128)}, u32[]{:S(2)}) copy-start(f32[2,768,1]{1,0,2:T(2,128)} %copy-done.18) | copy-start | bytes 18436
  884.1 199.2 %copy-start.15 = (f32[2,768]{1,0:T(2,128)S(1)}, f32[2,768]{1,0:T(2,128)}, u32[]{:S(2)}) copy-start(f32[2,768]{1,0:T(2,128)} %copy-done.13) | copy-start | bytes 18436
  1079.6 86.1 %all-to-all-start = ((f32[1,2,32,4,384]{4,2,1,0,3:T(8,128)}), f32[1,2,32,4,384]{4,2,1,0,3:T(8,128)S(1)}, u32[]{:S(2)}, u32[]{:S(2)}) async-start(f32[1,2,32,4,384]{4,2,1,0,3:T(8,128)} %copy.147), calls=%async_computation | async-start | bytes 786432 | tf_op jit(solution)/shard_map/all_to_all | solution.py:81
  1088.0 92.1 %copy-start.21 = (f32[2,768]{1,0:T(2,128)S(1)}, f32[2,768]{1,0:T(2,128)}, u32[]{:S(2)}) copy-start(f32[2,768]{1,0:T(2,128)} %copy-done.20) | copy-start | bytes 18436
  (20 other events, 139.6 us)
where the time goes:
time: 1190 us; the launch traced here: 1180 us
  other arithmetic  791 us (66%)
  blocking collectives  178 us (15%)
  matrix products  113 us (9%)
  local copies, waits for them, and re-layouts  88.5 us (7%)
    another operation x47, other arithmetic, per_device(): factor = jnp.linalg.cholesky(system)  505 us
    another operation x22, other arithmetic, per_device(): lax.linalg.triangular_solve(factor, forward[:, :, None], left_side=True,...  251 us
    psum x2, blocking collectives, per_device(): totals = lax.psum(stat_row, 'samp')  133 us
    another operation x20, matrix products, per_device(): factor = jnp.linalg.cholesky(system)  46.3 us
    another operation x45, local copies, waits for them, and re-layouts, per_device(): lax.linalg.triangular_solve(factor, forward[:, :, None], left_side=True,...  45.6 us
    another operation x22, matrix products, per_device(): lax.linalg.triangular_solve(factor, targets[:, :, None], left_side=True,...  28.6 us
    another operation x22, matrix products, per_device(): lax.linalg.triangular_solve(factor, forward[:, :, None], left_side=True,...  28.2 us
  transfers between devices with their start and end apart: 1, of which 0 were waited for; matrix products, arithmetic and copies ran while one was open for 1% of the time, Pallas kernels for 0%

commit v1 on v0

--- a/solution.py
+++ b/solution.py
@@ -61,7 +61,9 @@
         stat_row = jnp.stack(
             [jnp.sum(misfit * misfit), jnp.sum(effect * effect * inverse * live_rows), local_live]
         )
-        totals = lax.psum(stat_row, "samp")
+        totals = stat_row
+        for hop in (1, 2, 4, 8, 16):
+            totals = totals + lax.ppermute(totals, "samp", [(dev, dev ^ hop) for dev in range(32)])
         variance = (totals[0] + totals[1] + 1.0) / (totals[2] + 1.0)
         pooled = lax.psum(weight * effect * effect / variance, "slab")
         live_total = totals[2]

time: 1190 us -> 1100 us (0.924)
  blocking collectives: 178 us -> 48.3 us
  waiting for transfers between devices: 0.01 us -> 18.2 us
  starting transfers between devices: 3.71 us -> 21.3 us
    psum x2 -> x0, blocking collectives: 133 us -> none  [per_device(): totals = lax.psum(stat_row, 'samp')]
    ppermute x0 -> x10, waiting for transfers between devices: none -> 18.2 us  [per_device(): lax.ppermute(totals, 'samp', [(dev, dev ^ hop) for dev in range(32)])]
    ppermute x0 -> x10, starting transfers between devices: none -> 17.7 us  [per_device(): lax.ppermute(totals, 'samp', [(dev, dev ^ hop) for dev in range(32)])]
  transfers between devices with their start and end apart: 1 -> 11, of which waited for: 0 -> 9; matrix products, arithmetic and copies ran while one was open for 1% -> 1% of each run, Pallas kernels for 0% -> 0%
where the time goes in v1:
time: 1100 us; the launch traced here: 1090 us
  other arithmetic  797 us (72%)
  matrix products  112 us (10%)
  local copies, waits for them, and re-layouts  87 us (8%)
  blocking collectives  48.3 us (4%)
  starting transfers between devices  21.3 us (2%)
  waiting for transfers between devices  18.2 us (2%)
    another operation x47, other arithmetic, per_device(): factor = jnp.linalg.cholesky(system)  505 us
    another operation x22, other arithmetic, per_device(): lax.linalg.triangular_solve(factor, forward[:, :, None], left_side=True,...  251 us
    another operation x20, matrix products, per_device(): factor = jnp.linalg.cholesky(system)  46.3 us
    another operation x45, local copies, waits for them, and re-layouts, per_device(): lax.linalg.triangular_solve(factor, forward[:, :, None], left_side=True,...  45.5 us
    another operation x22, matrix products, per_device(): lax.linalg.triangular_solve(factor, targets[:, :, None], left_side=True,...  28.8 us
    another operation x22, matrix products, per_device(): lax.linalg.triangular_solve(factor, forward[:, :, None], left_side=True,...  28.2 us
    all_gather x1, blocking collectives, per_device(): spread = lax.all_gather(stacked, 'samp', axis=1, tiled=True)  25.2 us
    psum x2, blocking collectives, per_device(): pooled = lax.psum(weight * effect * effect / variance, 'slab')  23.1 us
  transfers between devices with their start and end apart: 11, of which 9 were waited for; matrix products, arithmetic and copies ran while one was open for 1% of the time, Pallas kernels for 0%

profile of v1, /device:TPU:0, one launch (start us, length us, event | category | flops | bytes accessed | tf_op | source)
XLA Modules:
  0.0 1092.7 jit_solution(10772897058031126667)
XLA Ops:
  28.3 23.5 %custom-call.57 = f32[2,128,128]{2,1,0:T(8,128)S(1)} custom-call(f32[2,128,128]{2,1,0:T(8,128)S(1)} %cholesky.662), custom_call_target="Cholesky" | custom-call | tf_op jit(solution)/shard_map/jit(cholesky)/cholesky | solution.py:47
  51.8 19.7 %custom-call.58 = f32[2,1,128,128]{2,3,1,0:T(8,128)S(1)} custom-call(f32[2,1,128,128]{3,2,1,0:T(8,128)S(1)} %select_bitcast_fusion.9), custom_call_target="InvertDiagBlocksLowerTriangular" | custom-call | tf_op jit(solution)/shard_map/jit(cholesky)/cholesky | solution.py:47
  79.4 23.6 %custom-call.59 = f32[2,128,128]{2,1,0:T(8,128)S(1)} custom-call(f32[2,128,128]{2,1,0:T(8,128)S(1)} %cholesky.666), custom_call_target="Cholesky" | custom-call | tf_op jit(solution)/shard_map/jit(cholesky)/cholesky | solution.py:47
  129.3 23.5 %custom-call.61 = f32[2,128,128]{2,1,0:T(8,128)S(1)} custom-call(f32[2,128,128]{2,1,0:T(8,128)S(1)} %cholesky.671), custom_call_target="Cholesky" | custom-call | tf_op jit(solution)/shard_map/jit(cholesky)/cholesky | solution.py:47
  153.6 20.7 %custom-call.62 = f32[2,1,128,128]{2,3,1,0:T(8,128)S(1)} custom-call(f32[2,1,128,128]{3,2,1,0:T(8,128)} %get-tuple-element.93), custom_call_target="InvertDiagBlocksLowerTriangular" | custom-call | tf_op jit(solution)/shard_map/jit(cholesky)/cholesky | solution.py:47
  179.9 24.9 %custom-call.63 = f32[2,128,128]{2,1,0:T(8,128)} custom-call(f32[2,128,128]{2,1,0:T(8,128)} %cholesky.676), custom_call_target="Cholesky" | custom-call | tf_op jit(solution)/shard_map/jit(cholesky)/cholesky | solution.py:47
  206.5 21.1 %custom-call.64 = f32[2,1,128,128]{2,3,1,0:T(8,128)} custom-call(f32[2,1,128,128]{3,2,1,0:T(8,128)} %get-tuple-element.91), custom_call_target="InvertDiagBlocksLowerTriangular" | custom-call | tf_op jit(solution)/shard_map/jit(cholesky)/cholesky | solution.py:47
  232.8 24.6 %custom-call.65 = f32[2,128,128]{2,1,0:T(8,128)S(1)} custom-call(f32[2,128,128]{2,1,0:T(8,128)} %cholesky.681), custom_call_target="Cholesky" | custom-call | tf_op jit(solution)/shard_map/jit(cholesky)/cholesky | solution.py:47
  258.2 21.1 %custom-call.66 = f32[2,1,128,128]{2,3,1,0:T(8,128)} custom-call(f32[2,1,128,128]{3,2,1,0:T(8,128)} %get-tuple-element.89), custom_call_target="InvertDiagBlocksLowerTriangular" | custom-call | tf_op jit(solution)/shard_map/jit(cholesky)/cholesky | solution.py:47
  283.3 23.5 %custom-call.67 = f32[2,128,128]{2,1,0:T(8,128)S(1)} custom-call(f32[2,128,128]{2,1,0:T(8,128)S(1)} %convolution_subtract_fusion.9), custom_call_target="Cholesky" | custom-call | tf_op jit(solution)/shard_map/jit(cholesky)/cholesky | solution.py:47
  315.4 22.0 %while.8 = (s32[]{:T(128)}, f32[2,768,768]{2,1,0:T(8,128)}, s32[6,2]{0,1:T(2,128)S(1)}, f32[6,2,128,128]{3,2,0,1:T(8,128)}, s32[]{:T(128)}) while((s32[]{:T(128)}, f32[2,768,768]{2,1,0:T(8,128)}, s32[6,2]{0,1:T(2,128)S(1)}, f32[6,2,128,128]{3,2,0,1:T(8,128)}, s32[]{:T(128)}) %tuple.92), condition=%wide.while_cond.1, body=%wide.while_body.1.sunk | while | flops 2 | bytes 263777 | solution.py:56
  337.5 119.5 %custom-call.69 = f32[2,6,128,128]{2,3,1,0:T(8,128)} custom-call(f32[2,6,128,128]{3,2,1,0:T(8,128)} %bitcast.493), custom_call_target="InvertDiagBlocksLowerTriangular" | custom-call | tf_op jit(solution)/shard_map/triangular_solve/custom-call.12 | solution.py:56
  552.0 23.5 %custom-call.70 = f32[2,128,128]{2,1,0:T(8,128)S(1)} custom-call(f32[2,128,128]{2,1,0:T(8,128)S(1)} %cholesky.685), custom_call_target="Cholesky" | custom-call | tf_op jit(solution)/shard_map/jit(cholesky)/cholesky | solution.py:47
  603.1 23.9 %custom-call.72 = f32[2,128,128]{2,1,0:T(8,128)S(1)} custom-call(f32[2,128,128]{2,1,0:T(8,128)S(1)} %cholesky.689), custom_call_target="Cholesky" | custom-call | tf_op jit(solution)/shard_map/jit(cholesky)/cholesky | solution.py:47
  653.2 23.5 %custom-call.74 = f32[2,128,128]{2,1,0:T(8,128)S(1)} custom-call(f32[2,128,128]{2,1,0:T(8,128)S(1)} %cholesky.694), custom_call_target="Cholesky" | custom-call | tf_op jit(solution)/shard_map/jit(cholesky)/cholesky | solution.py:47
  677.4 20.6 %custom-call.75 = f32[2,1,128,128]{2,3,1,0:T(8,128)S(1)} custom-call(f32[2,1,128,128]{3,2,1,0:T(8,128)} %get-tuple-element.84), custom_call_target="InvertDiagBlocksLowerTriangular" | custom-call | tf_op jit(solution)/shard_map/jit(cholesky)/cholesky | solution.py:47
  703.7 24.9 %custom-call.76 = f32[2,128,128]{2,1,0:T(8,128)} custom-call(f32[2,128,128]{2,1,0:T(8,128)} %cholesky.699), custom_call_target="Cholesky" | custom-call | tf_op jit(solution)/shard_map/jit(cholesky)/cholesky | solution.py:47
  730.3 21.1 %custom-call.77 = f32[2,1,128,128]{2,3,1,0:T(8,128)} custom-call(f32[2,1,128,128]{3,2,1,0:T(8,128)} %get-tuple-element.82), custom_call_target="InvertDiagBlocksLowerTriangular" | custom-call | tf_op jit(solution)/shard_map/jit(cholesky)/cholesky | solution.py:47
  756.5 24.5 %custom-call.78 = f32[2,128,128]{2,1,0:T(8,128)S(1)} custom-call(f32[2,128,128]{2,1,0:T(8,128)} %cholesky.704), custom_call_target="Cholesky" | custom-call | tf_op jit(solution)/shard_map/jit(cholesky)/cholesky | solution.py:47
  781.8 21.1 %custom-call.79 = f32[2,1,128,128]{2,3,1,0:T(8,128)} custom-call(f32[2,1,128,128]{3,2,1,0:T(8,128)} %get-tuple-element.80), custom_call_target="InvertDiagBlocksLowerTriangular" | custom-call | tf_op jit(solution)/shard_map/jit(cholesky)/cholesky | solution.py:47
  806.9 23.5 %custom-call.80 = f32[2,128,128]{2,1,0:T(8,128)S(1)} custom-call(f32[2,128,128]{2,1,0:T(8,128)S(1)} %convolution_subtract_fusion.8), custom_call_target="Cholesky" | custom-call | tf_op jit(solution)/shard_map/jit(cholesky)/cholesky | solution.py:47
  839.3 21.4 %while.9 = (s32[]{:T(128)}, f32[2,768,768]{2,1,0:T(8,128)}, s32[6,2]{0,1:T(2,128)S(1)}, f32[6,2,128,128]{3,2,0,1:T(8,128)}, s32[]{:T(128)}) while((s32[]{:T(128)}, f32[2,768,768]{2,1,0:T(8,128)}, s32[6,2]{0,1:T(2,128)S(1)}, f32[6,2,128,128]{3,2,0,1:T(8,128)}, s32[]{:T(128)}) %tuple.98), condition=%wide.while_cond.1.clone, body=%wide.while_body.1.clone.sunk | while | flops 2 | bytes 263777 | solution.py:56
  860.7 119.7 %custom-call.82 = f32[2,6,128,128]{2,3,1,0:T(8,128)} custom-call(f32[2,6,128,128]{3,2,1,0:T(8,128)} %bitcast.492), custom_call_target="InvertDiagBlocksLowerTriangular" | custom-call | tf_op jit(solution)/shard_map/triangular_solve/custom-call.12 | solution.py:56
  1013.7 25.2 %all_gather.3 = f32[2,49152]{1,0:T(2,128)S(1)} all-gather(f32[2,1536]{1,0:T(2,128)S(1)} %pad_maximum_fusion), channel_id=1, replica_groups=mesh['samp'=32,'slab'=4] {'samp'}, dimensions={1}, use_global_device_ids=true | all-gather | bytes 405504 | tf_op jit(solution)/shard_map/all_gather | solution.py:81
  (383 shorter events, 387.9 us)
Async XLA Ops:
  0.6 1078.0 %copy-start = (bf16[128,12288]{1,0:T(8,128)(2,1)S(1)}, bf16[128,12288]{1,0:T(8,128)(2,1)}, u32[]{:S(2)}) copy-start(bf16[128,12288]{1,0:T(8,128)(2,1)} %param.18) | copy-start | bytes 9437188
  309.1 147.9 %copy-start.31 = (s32[2]{0:T(128)S(1)}, s32[2]{0:T(128)}, u32[]{:S(2)}) copy-start(s32[2]{0:T(128)} %param.15) | copy-start | bytes 28
  309.1 147.9 %copy-start.34 = (f32[2,768,1]{1,0,2:T(2,128)S(1)}, f32[2,768,1]{1,0,2:T(2,128)}, u32[]{:S(2)}) copy-start(f32[2,768,1]{1,0,2:T(2,128)} %reshape_squeeze.13) | copy-start | bytes 18436
  314.4 157.1 %copy-start.39 = (f32[4]{0:T(128)S(1)}, f32[4]{0:T(128)}, u32[]{:S(2)}) copy-start(f32[4]{0:T(128)} %param.17) | copy-start | bytes 52
  314.4 158.6 %copy-start.35 = (f32[2,1,1536]{2,1,0:T(1,128)S(1)}, f32[2,1,1536]{2,1,0:T(1,128)}, u32[]{:S(2)}) copy-start(f32[2,1,1536]{2,1,0:T(1,128)} %param.14) | copy-start | bytes 36868
  314.4 173.0 %copy-start.15 = (f32[2,768]{1,0:T(2,128)S(1)}, f32[2,768]{1,0:T(2,128)}, u32[]{:S(2)}) copy-start(f32[2,768]{1,0:T(2,128)} %copy-done.14) | copy-start | bytes 18436
  337.5 154.6 %copy-start.17 = (s32[6,2]{0,1:T(2,128)}, s32[6,2]{0,1:T(2,128)S(1)}, u32[]{:S(2)}) copy-start(s32[6,2]{0,1:T(2,128)S(1)} %get-tuple-element.228) | copy-start | bytes 148
  494.9 1.3 collective-permute-start
  498.2 3.6 collective-permute-start.1
  503.8 5.1 collective-permute-start.2
  508.9 3.6 collective-permute-start.3
  512.5 5.1 collective-permute-start.4
  832.9 147.5 %copy-start.37 = (f32[2,128,1]{1,0,2:T(2,128)S(1)}, f32[2,128,1]{1,0,2:T(2,128)}, u32[]{:S(2)}) copy-start(f32[2,128,1]{1,0,2:T(2,128)} %copy-done.36) | copy-start | bytes 3076
  832.9 150.0 %copy-start.28 = (f32[2,768,1]{1,0,2:T(2,128)S(1)}, f32[2,768,1]{1,0,2:T(2,128)}, u32[]{:S(2)}) copy-start(f32[2,768,1]{1,0,2:T(2,128)} %copy-done.27) | copy-start | bytes 18436
  838.3 156.8 %copy-start.32 = (s32[2]{0:T(128)S(1)}, s32[2]{0:T(128)}, u32[]{:S(2)}) copy-start(s32[2]{0:T(128)} %param.15) | copy-start | bytes 28
  838.3 156.8 %copy-start.33 = (f32[2,768,1]{1,0,2:T(2,128)S(1)}, f32[2,768,1]{1,0,2:T(2,128)}, u32[]{:S(2)}) copy-start(f32[2,768,1]{1,0,2:T(2,128)} %mul.175) | copy-start | bytes 18436
  838.3 171.2 %copy-start.16 = (f32[2,768]{1,0:T(2,128)S(1)}, f32[2,768]{1,0:T(2,128)}, u32[]{:S(2)}) copy-start(f32[2,768]{1,0:T(2,128)} %copy-done.14) | copy-start | bytes 18436
  1013.1 77.6 %copy-start.20 = (f32[2,768]{1,0:T(2,128)S(1)}, f32[2,768]{1,0:T(2,128)}, u32[]{:S(2)}) copy-start(f32[2,768]{1,0:T(2,128)} %copy-done.19) | copy-start | bytes 18436
  1041.8 34.1 %all-to-all-start = ((f32[1,2,32,4,384]{4,2,1,0,3:T(8,128)}), f32[1,2,32,4,384]{4,2,1,0,3:T(8,128)S(1)}, u32[]{:S(2)}, u32[]{:S(2)}) async-start(f32[1,2,32,4,384]{4,2,1,0,3:T(8,128)} %copy.147), calls=%async_computation | async-start | bytes 786432 | tf_op jit(solution)/shard_map/all_to_all | solution.py:83
  1048.9 1.2 collective-permute-start.5
  1052.1 3.6 collective-permute-start.6
  1057.7 5.1 collective-permute-start.7
  1062.7 3.6 collective-permute-start.8
  1066.3 5.1 collective-permute-start.9
  (29 other events, 583.9 us)
